TPU v7x, 128 devices: a whole 4x4x4 slice. The times are simulated.
128 devices in a mesh: freq: 4 (over z), tile: 32 (over y, x, core).
Axes of the slice: x: 4, y: 4, z: 4, core: 2. Of those that a mesh axis runs over, the one named last changes fastest.
Arguments:
- traces: bfloat16 [32768, 1024], P('tile'), may hold values from -6 to 6
- bins: int32 [32768], P('tile'), may hold values from 0 to 196607, as said below
- counts: int32 [32], P('tile'), may hold values from 512 to 1024, as said below
- delay: float32 [2, 384, 512], P(None, 'tile'), may hold values from 0.02 to 0.06
- coeffs: float32 [2, 9, 256], P(None, None, 'freq'), may hold values from -1.4 to 1.4
Outputs:
- image: float32 [2, 384, 512], P(None, 'tile', 'freq')
Inputs may be any that keep to these rules, and one draw needn't show every extreme that they name: `bins`: only the first counts[o] trace slots of owner o are used; among them at most 80 fall in the 6144 cells of any one tile (rows x * 12 to x * 12 + 11), and in every draw some tile receives exactly 80 live traces from every owner. `counts`: some owner has all 1024 slots live.
All inputs are finite; a program needn't handle non-finite values.
Results may differ from a plain program's by a relative error of at most 0.0037.
Values may be sent and summed in bfloat16 or wider, within the bound.
No kernel may reach another device: no remote copies, remote signals or barrier semaphores. Data moves between devices by JAX's collectives and lax.ppermute only.
A program may use at most 320 MiB of HBM per device.

v0:
```python
import math

import jax
import jax.numpy as jnp
from jax import lax
from jax.sharding import PartitionSpec as P

NF = 256
ORDER = 8
DEPTHS = 2


def extended(cells, sides, width):
    for axis, dim in sides:
        count = lax.axis_size(axis)
        ends = count - 1
        head = lax.slice_in_dim(cells, 0, width, axis=dim)
        tail = lax.slice_in_dim(cells, cells.shape[dim] - width, cells.shape[dim], axis=dim)
        cells = jnp.concatenate(
            [
                lax.ppermute(tail, axis, [(i, (i + 1) % count) for i in range(ends)]),
                cells,
                lax.ppermute(head, axis, [((i + 1) % count, i) for i in range(ends)]),
            ],
            axis=dim,
        )
    return cells


def in_blocks(shard, dim, count):
    shape = shard.shape
    tiles = shard.reshape(*shape[:dim], count, shape[dim] // count, *shape[dim + 1 :])
    return jnp.moveaxis(tiles, dim, 0)


def summed_on_arrival(shard, axis, dim):
    count = lax.axis_size(axis)
    tiles = lax.all_to_all(in_blocks(shard, dim, count), axis, 0, 0, tiled=True)
    return jnp.sum(tiles, axis=0)


def stencil(padded):
    middle = padded[:, :, 1:-1]
    along_x = 0.5 * middle + 0.25 * (padded[:, :, 2:] + padded[:, :, :-2])
    edged = jnp.pad(along_x, ((0, 0), (0, 0), (0, 0), (1, 1)))
    along_y = 0.5 * along_x + 0.25 * (edged[:, :, :, 2:] + edged[:, :, :, :-2])
    return 2.0 * along_y - middle


def weigh(coef, index, field):
    real_part = coef[0, index][:, None, None]
    imag_part = coef[1, index][:, None, None]
    return jnp.stack(
        [real_part * field[0] - imag_part * field[1], real_part * field[1] + imag_part * field[0]]
    )


def apply_single(field):
    return stencil(extended(field, (("tile", 2),), 1))


def rotate(field, wave, delay_depth):
    phase = wave[:, None, None] * delay_depth[None]
    cosine = jnp.cos(phase)
    sine = jnp.sin(phase)
    return jnp.stack([cosine * field[0] - sine * field[1], sine * field[0] + cosine * field[1]])


def per_device(traces, bins, counts, delay, coeffs):
    tile_count = lax.axis_size("tile")
    freq_dev = coeffs.shape[2]
    rows_x = delay.shape[1]
    cols_y = delay.shape[2]
    cell_count = rows_x * cols_y
    trace_rows = traces.shape[0]
    samples = traces.shape[1]
    trace_ids = jnp.arange(trace_rows, dtype=jnp.int32)
    alive_mask = trace_ids < counts[0]
    slot_cap = trace_rows * 5 // (2 * tile_count)
    buffer_rows = tile_count * slot_cap
    freq_index = lax.axis_index("freq") * freq_dev + jnp.arange(freq_dev, dtype=jnp.int32) + 1
    turns = jnp.arange(samples, dtype=jnp.int32)[:, None] * freq_index[None, :] % samples
    angle = turns.astype(jnp.float32) * (2.0 * math.pi / samples)
    table = (
        jnp.concatenate([jnp.cos(angle), -jnp.sin(angle)], axis=1) / math.sqrt(samples)
    ).astype(jnp.bfloat16)
    spectra = jnp.dot(traces, table, preferred_element_type=jnp.float32).astype(jnp.bfloat16)
    dest_tile = bins // cell_count
    cell_local = bins - dest_tile * cell_count
    dest_onehot = (
        (dest_tile[:, None] == jnp.arange(tile_count, dtype=jnp.int32)[None, :])
        & alive_mask[:, None]
    ).astype(jnp.int32)
    running = jnp.cumsum(dest_onehot, axis=0) - 1
    slot_index = jnp.sum(running * dest_onehot, axis=1)
    position = jnp.where(alive_mask, dest_tile * slot_cap + slot_index, buffer_rows)
    source = (
        jnp.full((buffer_rows,), trace_rows, jnp.int32).at[position].set(trace_ids, mode="drop")
    )
    padded_rows = jnp.concatenate([spectra, jnp.zeros((1, spectra.shape[1]), jnp.bfloat16)], axis=0)
    padded_cells = jnp.concatenate([cell_local, jnp.full((1,), -1, jnp.int32)], axis=0)
    send_rows = padded_rows[source].reshape(tile_count, slot_cap, spectra.shape[1])
    send_cells = padded_cells[source].reshape(tile_count, slot_cap)
    recv_rows, recv_cells = (
        lax.all_to_all(send_rows, "tile", split_axis=0, concat_axis=0, tiled=True),
        lax.all_to_all(send_cells, "tile", split_axis=0, concat_axis=0, tiled=True),
    )
    recv_rows = recv_rows.reshape(buffer_rows, spectra.shape[1])
    recv_cells = recv_cells.reshape(buffer_rows)
    block_rows = 512
    cell_ids = jnp.arange(cell_count, dtype=jnp.int32)

    def add_block(step, acc):
        start = step * block_rows
        rows_piece = lax.dynamic_slice_in_dim(recv_rows, start, block_rows, 0)
        cells_piece = lax.dynamic_slice_in_dim(recv_cells, start, block_rows, 0)
        onehot = (cell_ids[:, None] == cells_piece[None, :]).astype(jnp.bfloat16)
        return acc + jnp.dot(onehot, rows_piece, preferred_element_type=jnp.float32)

    stacked = lax.fori_loop(
        0,
        buffer_rows // block_rows,
        add_block,
        jnp.zeros((cell_count, spectra.shape[1]), jnp.float32),
    )
    field = stacked.reshape(rows_x, cols_y, 2, freq_dev).transpose(2, 3, 0, 1)
    wave = freq_index.astype(jnp.float32)
    partials = []
    for depth in range(DEPTHS):
        field = rotate(field, wave, delay[depth])
        total = weigh(coeffs, 0, field)
        previous = field
        current = apply_single(field)
        total = total + weigh(coeffs, 1, current)
        for order in range(2, ORDER + 1):
            upcoming = 2.0 * apply_single(current) - previous
            previous, current = (current, upcoming)
            total = total + weigh(coeffs, order, current)
        field = total
        partial_image = jnp.sum(total[0], axis=0) * (1.0 / math.sqrt(NF))
        partials.append(partial_image)
    return summed_on_arrival(jnp.stack(partials), "freq", 2)


def solution(mesh):
    in_specs = (P("tile", None), P("tile"), P("tile"), P(None, "tile", None), P(None, None, "freq"))
    out_specs = P(None, "tile", "freq")
    return jax.shard_map(
        per_device, mesh=mesh, in_specs=in_specs, out_specs=out_specs, check_vma=False
    )
```

profile of v0, /device:TPU:8, one launch (start us, length us, event | category | flops | bytes accessed | tf_op | source)
XLA Modules:
  0.0 459.2 jit_solution(15632050810826472105)
XLA Ops:
  1.6 9.0 %reduce-window.6 = s32[32,8,128]{2,1,0:T(8,128)S(1)} reduce-window(s32[32,8,128]{2,1,0:T(8,128)S(1)} %fusion.210, s32[]{:T(128)} %constant.85.clone.1), window={size=1x1x128 pad=0_0x0_0x127_0}, to_apply=%region_0.1 | reduce-window | flops 4161536 | bytes 262148 | tf_op jit(solution)/shard_map/reduce-window
  16.2 13.6 %gather_fusion = s32[2560]{0:T(1024)S(1)} fusion(s32[1025]{0:T(1024)S(1)} %pad_add_fusion, s32[3072]{0:T(1024)S(1)} %pad_clamp_fusion), kind=kCustom, calls=%fused_computation | custom fusion | bytes 30720 | tf_op jit(solution)/shard_map/gather | solution.py:103
  30.5 7.5 %all-to-all-start = ((s32[32,1,80]{2,1,0:T(1,128)}), s32[32,1,80]{2,1,0:T(1,128)S(1)}, u32[]{:S(2)}, u32[]{:S(2)}) async-start(s32[32,1,80]{2,1,0:T(1,128)} %all_to_all.12), calls=%async_computation | async-start | bytes 32768 | tf_op jit(solution)/shard_map/all_to_all | solution.py:106
  41.5 6.1 %gather_fusion.1 = bf16[2560,128]{1,0:T(8,128)(2,1)} fusion(bf16[1025,128]{1,0:T(8,128)(2,1)S(1)} %concatenate.124.clone, s32[3072]{0:T(1024)S(1)} %pad_clamp_fusion), kind=kCustom, calls=%fused_computation.1 | custom fusion | bytes 1320960 | tf_op jit(solution)/shard_map/gather | solution.py:102
  47.6 7.4 %all-to-all-start.1 = ((bf16[32,80,128]{2,1,0:T(8,128)(2,1)}), bf16[32,80,128]{2,1,0:T(8,128)(2,1)S(1)}, u32[]{:S(2)}, u32[]{:S(2)}) async-start(bf16[32,80,128]{2,1,0:T(8,128)(2,1)} %bitcast.7), calls=%async_computation.1 | async-start | bytes 1310720 | tf_op jit(solution)/shard_map/all_to_all | solution.py:105
  56.3 9.5 %all-to-all-done.1 = bf16[32,80,128]{2,1,0:T(8,128)(2,1)S(1)} async-done(((bf16[32,80,128]{2,1,0:T(8,128)(2,1)}), bf16[32,80,128]{2,1,0:T(8,128)(2,1)S(1)}, u32[]{:S(2)}, u32[]{:S(2)}) %all-to-all-start.1) | async-done | bytes 655392 | tf_op jit(solution)/shard_map/all_to_all | solution.py:105
  65.7 27.0 %while.14 = (s32[]{:T(128)}, f32[6144,128]{1,0:T(8,128)}, s32[2560]{0:T(1024)S(1)}, bf16[2560,128]{1,0:T(8,128)(2,1)S(1)}, s32[]{:T(128)}, /*index=5*/s32[]{:T(128)}, s32[]{:T(128)}, s32[]{:T(128)}) while((s32[]{:T(128)}, f32[6144,128]{1,0:T(8,128)}, s32[2560]{0:T(1024)S(1)}, bf16[2560,128]{1,0:T(8,128)(2,1)S(1)}, s32[]{:T(128)}, ...), condition=%wide.region_5.6_spmd.clone, body=%wide.region_4.5_spmd.clone.sunk | while | flops 810024960 | bytes 6428829 | solution.py:120
  69.7 5.7 %fusion.241 = f32[6144,128]{1,0:T(8,128)} fusion(s32[512]{0:T(512)S(1)} %dynamic_slice.21, f32[6144,128]{1,0:T(8,128)} %get-tuple-element.260, pred[]{:T(512)S(6)} %compare.21, bf16[2560,128]{1,0:T(8,128)(2,1)S(1)} %get-tuple-element.270, s32[]{:T(128)S(6)} %select_n.57), kind=kOutput, calls=%fused_computation.6.clone.1 | convolution fusion | flops 810024960 | bytes 6424581 | tf_op jit(solution)/shard_map/while/body/eval_jaxpr/dot_general | solution.py:118
  75.5 5.7 %fusion.241 = f32[6144,128]{1,0:T(8,128)} fusion(s32[512]{0:T(512)S(1)} %dynamic_slice.21, f32[6144,128]{1,0:T(8,128)} %get-tuple-element.260, pred[]{:T(512)S(6)} %compare.21, bf16[2560,128]{1,0:T(8,128)(2,1)S(1)} %get-tuple-element.270, s32[]{:T(128)S(6)} %select_n.57), kind=kOutput, calls=%fused_computation.6.clone.1 | convolution fusion | flops 810024960 | bytes 6424581 | tf_op jit(solution)/shard_map/while/body/eval_jaxpr/dot_general | solution.py:118
  81.2 5.7 %fusion.241 = f32[6144,128]{1,0:T(8,128)} fusion(s32[512]{0:T(512)S(1)} %dynamic_slice.21, f32[6144,128]{1,0:T(8,128)} %get-tuple-element.260, pred[]{:T(512)S(6)} %compare.21, bf16[2560,128]{1,0:T(8,128)(2,1)S(1)} %get-tuple-element.270, s32[]{:T(128)S(6)} %select_n.57), kind=kOutput, calls=%fused_computation.6.clone.1 | convolution fusion | flops 810024960 | bytes 6424581 | tf_op jit(solution)/shard_map/while/body/eval_jaxpr/dot_general | solution.py:118
  87.0 5.7 %fusion.241 = f32[6144,128]{1,0:T(8,128)} fusion(s32[512]{0:T(512)S(1)} %dynamic_slice.21, f32[6144,128]{1,0:T(8,128)} %get-tuple-element.260, pred[]{:T(512)S(6)} %compare.21, bf16[2560,128]{1,0:T(8,128)(2,1)S(1)} %get-tuple-element.270, s32[]{:T(128)S(6)} %select_n.57), kind=kOutput, calls=%fused_computation.6.clone.1 | convolution fusion | flops 810024960 | bytes 6424581 | tf_op jit(solution)/shard_map/while/body/eval_jaxpr/dot_general | solution.py:118
  96.3 4.9 %reshape.127 = f32[12,512,2,64]{1,0,3,2:T(8,128)} reshape(f32[6144,128]{0,1:T(8,128)} %copy.30) | data formatting | bytes 6291456 | tf_op jit(solution)/shard_map/reshape | solution.py:126
  101.2 11.2 %multiply_subtract_fusion.17 = (f32[1,64,12,512]{3,2,1,0:T(8,128)}, f32[1,64,12,512]{3,2,1,0:T(8,128)S(1)}, f32[1,64,12,512]{3,2,1,0:T(8,128)S(1)}) fusion(f32[64]{0:T(128)S(1)} %get-tuple-element.213, f32[64]{0:T(128)S(1)} %get-tuple-element.214, f32[2,64,12,512]{3,2,1,0:T(8,128)} %bitcast.71, f32[12,512]{1,0:T(8,128)S(1)} %get-tuple-element.225, ...), kind=kLoop, calls=%fused_computation.319 | loop fusion | flops 3932160 | bytes 7889664 | tf_op jit(solution)/shard_map/sub | solution.py:54
  113.0 5.2 %collective-permute-start = (f32[2,64,1,512]{3,2,1,0:T(1,128)S(1)}, f32[2,64,1,512]{3,2,1,0:T(1,128)S(1)}, u32[]{:S(2)}, u32[]{:S(2)}) collective-permute-start(f32[2,64,1,512]{3,2,1,0:T(1,128)S(1)} %get-tuple-element.194), channel_id=1, source_target_pairs={{1,0},{2,1},{3,2},{4,3},{5,4},{6,5},{7,6},{8,7},{9,8},{10,9},{11,1... | collective-permute-start | bytes 786440 | tf_op jit(solution)/shard_map/ppermute | solution.py:23
  122.0 5.9 %collective-permute-done.1 = f32[2,64,1,512]{3,2,1,0:T(1,128)S(1)} collective-permute-done((f32[2,64,1,512]{3,2,1,0:T(1,128)S(1)}, f32[2,64,1,512]{3,2,1,0:T(1,128)S(1)}, u32[]{:S(2)}, u32[]{:S(2)}) %collective-permute-start.1) | collective-permute-done | bytes 262176 | tf_op jit(solution)/shard_map/ppermute | solution.py:21
  140.0 4.9 %collective-permute-done.3 = f32[2,64,1,512]{3,2,1,0:T(1,128)S(1)} collective-permute-done((f32[2,64,1,512]{3,2,1,0:T(1,128)S(1)}, f32[2,64,1,512]{3,2,1,0:T(1,128)S(1)}, u32[]{:S(2)}, u32[]{:S(2)}) %collective-permute-start.3) | collective-permute-done | bytes 262176 | tf_op jit(solution)/shard_map/ppermute | solution.py:21
  167.0 11.2 %fusion.25 = f32[2,64,12,512]{3,2,1,0:T(8,128)S(1)} fusion(f32[2,64,12,512]{3,2,1,0:T(8,128)S(1)} %fusion.18, f32[2,64,12,512]{3,2,1,0:T(8,128)} %fusion.156, f32[1,64,12,512]{3,2,1,0:T(8,128)S(1)} %get-tuple-element.129, f32[1,64,12,512]{3,2,1,0:T(8,128)S(1)} %get-tuple-element.130, f32[2,64,12,512]{3,2,1,0:T(8,128)} %copy-done.4), kind=kLoop, calls=%fused_computation.70 | loop fusion | flops 11796480 | bytes 15728640 | tf_op jit(solution)/shard_map/sub | solution.py:136
  268.8 11.8 %fusion.169 = f32[2,64,12,512]{3,2,1,0:T(8,128)S(1)} fusion(f32[1,64,12,512]{3,2,1,0:T(8,128)} %multiply_add_fusion.17, f32[1,64,12,512]{3,2,1,0:T(8,128)} %get-tuple-element.128, f32[1,64,12,512]{3,2,1,0:T(8,128)S(1)} %copy-done.7, f32[1,64,12,512]{3,2,1,0:T(8,128)S(1)} %copy-done.6, f32[1,64,12,512]{3,2,1,0:T(8,128)S(1)} %copy-done.9, ...), kind=kLoop, calls=%fused_computation.251 | loop fusion | flops 13369344 | bytes 31457280 | tf_op jit(solution)/shard_map/add | solution.py:138
  280.6 9.6 %multiply_subtract_fusion.8 = (f32[1,64,12,512]{3,2,1,0:T(8,128)}, f32[1,64,12,512]{3,2,1,0:T(8,128)S(1)}, f32[1,64,12,512]{3,2,1,0:T(8,128)}, f32[12,512]{1,0:T(8,128)S(1)}) fusion(f32[64]{0:T(128)S(1)} %get-tuple-element.213, f32[64]{0:T(128)S(1)} %get-tuple-element.214, f32[2,64,12,512]{3,2,1,0:T(8,128)S(1)} %fusion.169, ...), kind=kLoop, calls=%fused_computation.301 | loop fusion | flops 4319232 | bytes 7914240 | tf_op jit(solution)/shard_map/sub | solution.py:54
  298.4 5.7 %collective-permute-done.17 = f32[2,64,1,512]{3,2,1,0:T(1,128)S(1)} collective-permute-done((f32[2,64,1,512]{3,2,1,0:T(1,128)S(1)}, f32[2,64,1,512]{3,2,1,0:T(1,128)S(1)}, u32[]{:S(2)}, u32[]{:S(2)}) %collective-permute-start.17) | collective-permute-done | bytes 262176 | tf_op jit(solution)/shard_map/ppermute | solution.py:21
  344.1 11.1 %fusion.79 = f32[2,64,12,512]{3,2,1,0:T(8,128)S(1)} fusion(f32[2,64,12,512]{3,2,1,0:T(8,128)S(1)} %fusion.72, f32[2,64,12,512]{3,2,1,0:T(8,128)} %fusion.132, f32[1,64,12,512]{3,2,1,0:T(8,128)S(1)} %get-tuple-element.126, f32[1,64,12,512]{3,2,1,0:T(8,128)S(1)} %copy-done.2, f32[2,64,12,512]{3,2,1,0:T(8,128)} %copy-done.3), kind=kLoop, calls=%fused_computation.124 | loop fusion | flops 11796480 | bytes 15728640 | tf_op jit(solution)/shard_map/sub | solution.py:136
  378.7 5.5 %collective-permute-done.25 = f32[2,64,1,512]{3,2,1,0:T(1,128)S(1)} collective-permute-done((f32[2,64,1,512]{3,2,1,0:T(1,128)S(1)}, f32[2,64,1,512]{3,2,1,0:T(1,128)S(1)}, u32[]{:S(2)}, u32[]{:S(2)}) %collective-permute-start.25) | collective-permute-done | bytes 262176 | tf_op jit(solution)/shard_map/ppermute | solution.py:21
  395.2 5.9 %collective-permute-done.27 = f32[2,64,1,512]{3,2,1,0:T(1,128)S(1)} collective-permute-done((f32[2,64,1,512]{3,2,1,0:T(1,128)S(1)}, f32[2,64,1,512]{3,2,1,0:T(1,128)S(1)}, u32[]{:S(2)}, u32[]{:S(2)}) %collective-permute-start.27) | collective-permute-done | bytes 262176 | tf_op jit(solution)/shard_map/ppermute | solution.py:21
  447.8 10.7 %all_to_all.19 = f32[4,2,12,128]{3,1,2,0:T(2,128)S(1)} all-to-all(f32[4,2,12,128]{3,1,2,0:T(2,128)S(1)} %copy.32), channel_id=1, replica_groups=mesh['freq'=4,'tile'=32] {'freq'}, dimensions={0} | all-to-all | bytes 98304 | tf_op jit(solution)/shard_map/all_to_all | solution.py:38
  (207 shorter events, 277.4 us)
Async XLA Ops:
  30.5 17.1 %all-to-all-start = ((s32[32,1,80]{2,1,0:T(1,128)}), s32[32,1,80]{2,1,0:T(1,128)S(1)}, u32[]{:S(2)}, u32[]{:S(2)}) async-start(s32[32,1,80]{2,1,0:T(1,128)} %all_to_all.12), calls=%async_computation | async-start | bytes 32768 | tf_op jit(solution)/shard_map/all_to_all | solution.py:106
  47.6 18.2 %all-to-all-start.1 = ((bf16[32,80,128]{2,1,0:T(8,128)(2,1)}), bf16[32,80,128]{2,1,0:T(8,128)(2,1)S(1)}, u32[]{:S(2)}, u32[]{:S(2)}) async-start(bf16[32,80,128]{2,1,0:T(8,128)(2,1)} %bitcast.7), calls=%async_computation.1 | async-start | bytes 1310720 | tf_op jit(solution)/shard_map/all_to_all | solution.py:105
  113.0 9.1 %collective-permute-start = (f32[2,64,1,512]{3,2,1,0:T(1,128)S(1)}, f32[2,64,1,512]{3,2,1,0:T(1,128)S(1)}, u32[]{:S(2)}, u32[]{:S(2)}) collective-permute-start(f32[2,64,1,512]{3,2,1,0:T(1,128)S(1)} %get-tuple-element.194), channel_id=1, source_target_pairs={{1,0},{2,1},{3,2},{4,3},{5,4},{6,5},{7,6},{8,7},{9,8},{10,9},{11,1... | collective-permute-start | bytes 786440 | tf_op jit(solution)/shard_map/ppermute | solution.py:23
  118.1 9.8 %collective-permute-start.1 = (f32[2,64,1,512]{3,2,1,0:T(1,128)S(1)}, f32[2,64,1,512]{3,2,1,0:T(1,128)S(1)}, u32[]{:S(2)}, u32[]{:S(2)}) collective-permute-start(f32[2,64,1,512]{3,2,1,0:T(1,128)S(1)} %get-tuple-element.195), channel_id=1, source_target_pairs={{0,1},{1,2},{2,3},{3,4},{4,5},{5,6},{6,7},{7,8},{8,9},{9,10},{10,1... | collective-permute-start | bytes 786440 | tf_op jit(solution)/shard_map/ppermute | solution.py:21
  135.2 9.8 %collective-permute-start.3 = (f32[2,64,1,512]{3,2,1,0:T(1,128)S(1)}, f32[2,64,1,512]{3,2,1,0:T(1,128)S(1)}, u32[]{:S(2)}, u32[]{:S(2)}) collective-permute-start(f32[2,64,1,512]{3,2,1,0:T(1,128)S(1)} %get-tuple-element.193), channel_id=1, source_target_pairs={{0,1},{1,2},{2,3},{3,4},{4,5},{5,6},{6,7},{7,8},{8,9},{9,10},{10,1... | collective-permute-start | bytes 786440 | tf_op jit(solution)/shard_map/ppermute | solution.py:21
  152.1 7.1 %collective-permute-start.4 = (f32[2,64,1,512]{3,2,1,0:T(1,128)S(1)}, f32[2,64,1,512]{3,2,1,0:T(1,128)S(1)}, u32[]{:S(2)}, u32[]{:S(2)}) collective-permute-start(f32[2,64,1,512]{3,2,1,0:T(1,128)S(1)} %get-tuple-element.190), channel_id=1, source_target_pairs={{1,0},{2,1},{3,2},{4,3},{5,4},{6,5},{7,6},{8,7},{9,8},{10,9},{11,1... | collective-permute-start | bytes 786440 | tf_op jit(solution)/shard_map/ppermute | solution.py:23
  154.0 9.8 %collective-permute-start.5 = (f32[2,64,1,512]{3,2,1,0:T(1,128)S(1)}, f32[2,64,1,512]{3,2,1,0:T(1,128)S(1)}, u32[]{:S(2)}, u32[]{:S(2)}) collective-permute-start(f32[2,64,1,512]{3,2,1,0:T(1,128)S(1)} %get-tuple-element.191), channel_id=1, source_target_pairs={{0,1},{1,2},{2,3},{3,4},{4,5},{5,6},{6,7},{7,8},{8,9},{9,10},{10,1... | collective-permute-start | bytes 786440 | tf_op jit(solution)/shard_map/ppermute | solution.py:21
  180.7 9.8 %collective-permute-start.7 = (f32[2,64,1,512]{3,2,1,0:T(1,128)S(1)}, f32[2,64,1,512]{3,2,1,0:T(1,128)S(1)}, u32[]{:S(2)}, u32[]{:S(2)}) collective-permute-start(f32[2,64,1,512]{3,2,1,0:T(1,128)S(1)} %get-tuple-element.189), channel_id=1, source_target_pairs={{0,1},{1,2},{2,3},{3,4},{4,5},{5,6},{6,7},{7,8},{8,9},{9,10},{10,1... | collective-permute-start | bytes 786440 | tf_op jit(solution)/shard_map/ppermute | solution.py:21
  197.5 9.8 %collective-permute-start.9 = (f32[2,64,1,512]{3,2,1,0:T(1,128)S(1)}, f32[2,64,1,512]{3,2,1,0:T(1,128)S(1)}, u32[]{:S(2)}, u32[]{:S(2)}) collective-permute-start(f32[2,64,1,512]{3,2,1,0:T(1,128)S(1)} %get-tuple-element.187), channel_id=1, source_target_pairs={{0,1},{1,2},{2,3},{3,4},{4,5},{5,6},{6,7},{7,8},{8,9},{9,10},{10,1... | collective-permute-start | bytes 786440 | tf_op jit(solution)/shard_map/ppermute | solution.py:21
  212.6 7.3 %collective-permute-start.10 = (f32[2,64,1,512]{3,2,1,0:T(1,128)S(1)}, f32[2,64,1,512]{3,2,1,0:T(1,128)S(1)}, u32[]{:S(2)}, u32[]{:S(2)}) collective-permute-start(f32[2,64,1,512]{3,2,1,0:T(1,128)S(1)} %get-tuple-element.184), channel_id=1, source_target_pairs={{1,0},{2,1},{3,2},{4,3},{5,4},{6,5},{7,6},{8,7},{9,8},{10,9},{11,1... | collective-permute-start | bytes 786440 | tf_op jit(solution)/shard_map/ppermute | solution.py:23
  214.5 9.8 %collective-permute-start.11 = (f32[2,64,1,512]{3,2,1,0:T(1,128)S(1)}, f32[2,64,1,512]{3,2,1,0:T(1,128)S(1)}, u32[]{:S(2)}, u32[]{:S(2)}) collective-permute-start(f32[2,64,1,512]{3,2,1,0:T(1,128)S(1)} %get-tuple-element.185), channel_id=1, source_target_pairs={{0,1},{1,2},{2,3},{3,4},{4,5},{5,6},{6,7},{7,8},{8,9},{9,10},{10,1... | collective-permute-start | bytes 786440 | tf_op jit(solution)/shard_map/ppermute | solution.py:21
  231.7 9.8 %collective-permute-start.13 = (f32[2,64,1,512]{3,2,1,0:T(1,128)S(1)}, f32[2,64,1,512]{3,2,1,0:T(1,128)S(1)}, u32[]{:S(2)}, u32[]{:S(2)}) collective-permute-start(f32[2,64,1,512]{3,2,1,0:T(1,128)S(1)} %get-tuple-element.183), channel_id=1, source_target_pairs={{0,1},{1,2},{2,3},{3,4},{4,5},{5,6},{6,7},{7,8},{8,9},{9,10},{10,1... | collective-permute-start | bytes 786440 | tf_op jit(solution)/shard_map/ppermute | solution.py:21
  249.0 9.8 %collective-permute-start.15 = (f32[2,64,1,512]{3,2,1,0:T(1,128)S(1)}, f32[2,64,1,512]{3,2,1,0:T(1,128)S(1)}, u32[]{:S(2)}, u32[]{:S(2)}) collective-permute-start(f32[2,64,1,512]{3,2,1,0:T(1,128)S(1)} %get-tuple-element.181), channel_id=1, source_target_pairs={{0,1},{1,2},{2,3},{3,4},{4,5},{5,6},{6,7},{7,8},{8,9},{9,10},{10,1... | collective-permute-start | bytes 786440 | tf_op jit(solution)/shard_map/ppermute | solution.py:21
  294.3 9.8 %collective-permute-start.17 = (f32[2,64,1,512]{3,2,1,0:T(1,128)S(1)}, f32[2,64,1,512]{3,2,1,0:T(1,128)S(1)}, u32[]{:S(2)}, u32[]{:S(2)}) collective-permute-start(f32[2,64,1,512]{3,2,1,0:T(1,128)S(1)} %get-tuple-element.179), channel_id=1, source_target_pairs={{0,1},{1,2},{2,3},{3,4},{4,5},{5,6},{6,7},{7,8},{8,9},{9,10},{10,1... | collective-permute-start | bytes 786440 | tf_op jit(solution)/shard_map/ppermute | solution.py:21
  309.3 7.1 %collective-permute-start.18 = (f32[2,64,1,512]{3,2,1,0:T(1,128)S(1)}, f32[2,64,1,512]{3,2,1,0:T(1,128)S(1)}, u32[]{:S(2)}, u32[]{:S(2)}) collective-permute-start(f32[2,64,1,512]{3,2,1,0:T(1,128)S(1)} %get-tuple-element.176), channel_id=1, source_target_pairs={{1,0},{2,1},{3,2},{4,3},{5,4},{6,5},{7,6},{8,7},{9,8},{10,9},{11,1... | collective-permute-start | bytes 786440 | tf_op jit(solution)/shard_map/ppermute | solution.py:23
  311.2 9.8 %collective-permute-start.19 = (f32[2,64,1,512]{3,2,1,0:T(1,128)S(1)}, f32[2,64,1,512]{3,2,1,0:T(1,128)S(1)}, u32[]{:S(2)}, u32[]{:S(2)}) collective-permute-start(f32[2,64,1,512]{3,2,1,0:T(1,128)S(1)} %get-tuple-element.177), channel_id=1, source_target_pairs={{0,1},{1,2},{2,3},{3,4},{4,5},{5,6},{6,7},{7,8},{8,9},{9,10},{10,1... | collective-permute-start | bytes 786440 | tf_op jit(solution)/shard_map/ppermute | solution.py:21
  328.8 7.6 %collective-permute-start.20 = (f32[2,64,1,512]{3,2,1,0:T(1,128)S(1)}, f32[2,64,1,512]{3,2,1,0:T(1,128)S(1)}, u32[]{:S(2)}, u32[]{:S(2)}) collective-permute-start(f32[2,64,1,512]{3,2,1,0:T(1,128)S(1)} %get-tuple-element.174), channel_id=1, source_target_pairs={{1,0},{2,1},{3,2},{4,3},{5,4},{6,5},{7,6},{8,7},{9,8},{10,9},{11,1... | collective-permute-start | bytes 786440 | tf_op jit(solution)/shard_map/ppermute | solution.py:23
  331.1 9.8 %collective-permute-start.21 = (f32[2,64,1,512]{3,2,1,0:T(1,128)S(1)}, f32[2,64,1,512]{3,2,1,0:T(1,128)S(1)}, u32[]{:S(2)}, u32[]{:S(2)}) collective-permute-start(f32[2,64,1,512]{3,2,1,0:T(1,128)S(1)} %get-tuple-element.175), channel_id=1, source_target_pairs={{0,1},{1,2},{2,3},{3,4},{4,5},{5,6},{6,7},{7,8},{8,9},{9,10},{10,1... | collective-permute-start | bytes 786440 | tf_op jit(solution)/shard_map/ppermute | solution.py:21
  355.8 7.3 %collective-permute-start.22 = (f32[2,64,1,512]{3,2,1,0:T(1,128)S(1)}, f32[2,64,1,512]{3,2,1,0:T(1,128)S(1)}, u32[]{:S(2)}, u32[]{:S(2)}) collective-permute-start(f32[2,64,1,512]{3,2,1,0:T(1,128)S(1)} %get-tuple-element.172), channel_id=1, source_target_pairs={{1,0},{2,1},{3,2},{4,3},{5,4},{6,5},{7,6},{8,7},{9,8},{10,9},{11,1... | collective-permute-start | bytes 786440 | tf_op jit(solution)/shard_map/ppermute | solution.py:23
  357.7 9.8 %collective-permute-start.23 = (f32[2,64,1,512]{3,2,1,0:T(1,128)S(1)}, f32[2,64,1,512]{3,2,1,0:T(1,128)S(1)}, u32[]{:S(2)}, u32[]{:S(2)}) collective-permute-start(f32[2,64,1,512]{3,2,1,0:T(1,128)S(1)} %get-tuple-element.173), channel_id=1, source_target_pairs={{0,1},{1,2},{2,3},{3,4},{4,5},{5,6},{6,7},{7,8},{8,9},{9,10},{10,1... | collective-permute-start | bytes 786440 | tf_op jit(solution)/shard_map/ppermute | solution.py:21
  374.5 9.8 %collective-permute-start.25 = (f32[2,64,1,512]{3,2,1,0:T(1,128)S(1)}, f32[2,64,1,512]{3,2,1,0:T(1,128)S(1)}, u32[]{:S(2)}, u32[]{:S(2)}) collective-permute-start(f32[2,64,1,512]{3,2,1,0:T(1,128)S(1)} %get-tuple-element.171), channel_id=1, source_target_pairs={{0,1},{1,2},{2,3},{3,4},{4,5},{5,6},{6,7},{7,8},{8,9},{9,10},{10,1... | collective-permute-start | bytes 786440 | tf_op jit(solution)/shard_map/ppermute | solution.py:21
  391.4 9.8 %collective-permute-start.27 = (f32[2,64,1,512]{3,2,1,0:T(1,128)S(1)}, f32[2,64,1,512]{3,2,1,0:T(1,128)S(1)}, u32[]{:S(2)}, u32[]{:S(2)}) collective-permute-start(f32[2,64,1,512]{3,2,1,0:T(1,128)S(1)} %get-tuple-element.169), channel_id=1, source_target_pairs={{0,1},{1,2},{2,3},{3,4},{4,5},{5,6},{6,7},{7,8},{8,9},{9,10},{10,1... | collective-permute-start | bytes 786440 | tf_op jit(solution)/shard_map/ppermute | solution.py:21
  408.6 9.8 %collective-permute-start.29 = (f32[2,64,1,512]{3,2,1,0:T(1,128)S(1)}, f32[2,64,1,512]{3,2,1,0:T(1,128)S(1)}, u32[]{:S(2)}, u32[]{:S(2)}) collective-permute-start(f32[2,64,1,512]{3,2,1,0:T(1,128)S(1)} %get-tuple-element.167), channel_id=1, source_target_pairs={{0,1},{1,2},{2,3},{3,4},{4,5},{5,6},{6,7},{7,8},{8,9},{9,10},{10,1... | collective-permute-start | bytes 786440 | tf_op jit(solution)/shard_map/ppermute | solution.py:21
  425.8 9.8 %collective-permute-start.31 = (f32[2,64,1,512]{3,2,1,0:T(1,128)S(1)}, f32[2,64,1,512]{3,2,1,0:T(1,128)S(1)}, u32[]{:S(2)}, u32[]{:S(2)}) collective-permute-start(f32[2,64,1,512]{3,2,1,0:T(1,128)S(1)} %get-tuple-element.165), channel_id=1, source_target_pairs={{0,1},{1,2},{2,3},{3,4},{4,5},{5,6},{6,7},{7,8},{8,9},{9,10},{10,1... | collective-permute-start | bytes 786440 | tf_op jit(solution)/shard_map/ppermute | solution.py:21
  (29 other events, 237.7 us)
where the time goes:
time: 468 us; the launch traced here: 459 us
  other arithmetic  193 us (41%)
  waiting for transfers between devices  89.8 us (19%)
  starting transfers between devices  88.9 us (19%)
  local copies, waits for them, and re-layouts  47.3 us (10%)
  matrix products  27.7 us (6%)
  blocking collectives  10.7 us (2%)
    ppermute x16, waiting for transfers between devices, extended(): lax.ppermute(tail, axis, [(i, (i + 1) % count) for i in range(ends)])  79.3 us
    sub x14, other arithmetic, per_device(): upcoming = 2.0 * apply_single(current) - previous  61.8 us
    sub x18, other arithmetic, weigh(): real_part * field[0] - imag_part * field[1]  54.9 us
    ppermute x16, starting transfers between devices, extended(): lax.ppermute(tail, axis, [(i, (i + 1) % count) for i in range(ends)])  39.6 us
    ppermute x16, starting transfers between devices, extended(): lax.ppermute(head, axis, [((i + 1) % count, i) for i in range(ends)])  34.4 us
    add x16, other arithmetic, stencil(): along_x = 0.5 * middle + 0.25 * (padded[:, :, 2:] + padded[:, :, :-2])  32.4 us
    dot_general x5, matrix products, add_block(): return acc + jnp.dot(onehot, rows_piece, preferred_element_type=jnp.float32)  26.6 us
    add x2, other arithmetic, per_device(): total = total + weigh(coeffs, order, current)  14.7 us
  transfers between devices with their start and end apart: 34, of which 18 were waited for; matrix products, arithmetic and copies ran while one was open for 10% of the time, Pallas kernels for 0%

commit v1 on v0

v1 whole, which is shorter than its diff:
```python
import functools
import math

import jax
import jax.numpy as jnp
import numpy as np
from jax import lax
from jax.experimental import pallas as pl
from jax.experimental.pallas import tpu as pltpu
from jax.sharding import PartitionSpec as P

NF = 256
ORDER = 8
DEPTHS = 2
SLOT = 80
BLOCK = 96
ROWS = 12
HALO = 8
NY = 512
TILES = 32
F32 = jnp.float32
BF16 = jnp.bfloat16
NT_DIMS = (((1,), (1,)), ((), ()))


def sine_basis():
    k = np.arange(1, NY + 1)
    basis = np.sqrt(2.0 / (NY + 1)) * np.sin(np.pi * np.outer(k, k) / (NY + 1))
    high = basis.astype(jnp.bfloat16)
    low = (basis - high.astype(np.float64)).astype(jnp.bfloat16)
    return np.concatenate([high, low], axis=0)


def shift_weights():
    k = np.arange(1, NY + 1)
    s = 0.5 + 0.5 * np.cos(np.pi * k / (NY + 1))
    wide = ORDER + 2

    def apply_g(poly):
        out = (s - 1.0) * poly
        for d in range(wide - 1):
            below = poly[abs(d - 1)]
            out[d] = out[d] + 0.5 * s * (below + poly[d + 1])
        return out

    terms = [np.zeros((wide, NY)) for _ in range(2)]
    terms[0][0] = 1.0
    terms[1] = apply_g(terms[0])
    for _ in range(2, ORDER + 1):
        terms.append(2.0 * apply_g(terms[-1]) - terms[-2])
    return np.stack(terms)[:, : ORDER + 1].astype(np.float32)


def pack_kernel(count_ref, bins_ref, traces_ref, table_ref, out_ref, spec_ref):
    slots = traces_ref.shape[0]
    bins = bins_ref[...]
    tile = ((bins.astype(F32) + 0.5) * (1.0 / (ROWS * NY))).astype(jnp.int32)
    local = bins - tile * (ROWS * NY)
    lane = lax.broadcasted_iota(jnp.int32, (1, slots), 1)
    alive = lane < count_ref[0]
    tile_of = lax.broadcasted_iota(jnp.int32, (TILES, slots), 0)
    hot = (tile_of == jnp.where(alive, tile, -1)).astype(F32)
    before = (
        lax.broadcasted_iota(jnp.int32, (slots, slots), 0)
        < lax.broadcasted_iota(jnp.int32, (slots, slots), 1)
    )
    before = jnp.where(before, 1.0, 0.0).astype(BF16)
    rank = jnp.dot(hot.astype(BF16), before, preferred_element_type=F32)
    place = jnp.sum(hot * (rank + (SLOT * tile_of).astype(F32)), axis=0, keepdims=True)
    place = jnp.where(alive, place.astype(jnp.int32), -1)

    spec_ref[:, :128] = jnp.dot(
        traces_ref[...], table_ref[...], preferred_element_type=F32
    ).astype(BF16)
    kind = lax.broadcasted_iota(jnp.int32, (8, slots), 0)
    code = jnp.where(
        kind == 0, (local >> 9) + 1, jnp.where(kind == 1, local & 255, (local >> 8) & 1)
    )
    code = jnp.where(kind < 3, code, 0).astype(F32)
    spec_ref[:, 128:] = jnp.transpose(jnp.concatenate([code] * 16, axis=0)).astype(BF16)

    group = 8
    lane_group = lax.broadcasted_iota(jnp.int32, (16, 128), 1) >> 3

    def body(step, _):
        base = step * (group * SLOT)
        slot = lax.broadcasted_iota(jnp.int32, (group * SLOT, slots), 0) + base
        pick = jnp.where(slot == place, 1.0, 0.0).astype(BF16)
        got = jnp.dot(pick, spec_ref[...], preferred_element_type=F32)
        for i in range(group):
            dest = step * group + i
            out_ref[dest, 0:SLOT, :] = got[SLOT * i : SLOT * (i + 1), :128].astype(BF16)
            codes = jnp.zeros((16, 128), F32)
            for g in range(5):
                piece = got[SLOT * i + 16 * g : SLOT * i + 16 * (g + 1), 128:]
                codes = jnp.where(lane_group == g, piece, codes)
            out_ref[dest, SLOT:BLOCK, :] = codes.astype(BF16)
        return 0

    lax.fori_loop(0, TILES // group, body, 0)


def pack(counts, bins, traces, table):
    slots = traces.shape[0]
    return pl.pallas_call(
        pack_kernel,
        out_shape=jax.ShapeDtypeStruct((TILES, BLOCK, 128), BF16),
        in_specs=[
            pl.BlockSpec(memory_space=pltpu.SMEM),
            pl.BlockSpec(memory_space=pltpu.VMEM),
            pl.BlockSpec(memory_space=pltpu.VMEM),
            pl.BlockSpec(memory_space=pltpu.VMEM),
        ],
        out_specs=pl.BlockSpec(memory_space=pltpu.VMEM),
        scratch_shapes=[pltpu.VMEM((slots, 256), BF16)],
        cost_estimate=pl.CostEstimate(
            flops=3_000_000_000, bytes_accessed=4_000_000, transcendentals=0
        ),
        compiler_params=pltpu.CompilerParams(vmem_limit_bytes=48 * 1024 * 1024),
        name="pack_traces",
    )(counts, bins.reshape(1, slots), traces, table)


def unpack(recv_ref, vals_ref, hot_ref, code_ref):
    chunk = 8 * SLOT

    def body(step, _):
        lanes = pl.ds(pl.multiple_of(step * chunk, 128), chunk)
        block = recv_ref[pl.ds(step * 8, 8)]
        vals = block[:, :SLOT, :].reshape(chunk, 128).astype(F32)
        vals_ref[:, lanes] = jnp.transpose(vals).astype(BF16)
        codes = block[:, SLOT:BLOCK, :].astype(F32)
        codes = jnp.concatenate([codes] * 5, axis=1).reshape(chunk, 128)
        codes = jnp.transpose(codes)
        k = lax.broadcasted_iota(jnp.int32, (8, chunk), 1)
        owner = ((k.astype(F32) + 0.5) * (1.0 / SLOT)).astype(jnp.int32)
        g_of = (k - owner * SLOT) >> 4
        code = jnp.zeros((8, chunk), F32)
        for g in range(5):
            code = jnp.where(g_of == g, codes[8 * g : 8 * (g + 1)], code)
        code_ref[:, lanes] = code
        y = (code[1:2] + 256.0 * code[2:3]).astype(jnp.int32)
        row = lax.broadcasted_iota(jnp.int32, (NY, chunk), 0)
        hot_ref[:, lanes] = jnp.where(row == y, 1.0, 0.0).astype(BF16)
        return 0

    lax.fori_loop(0, TILES // 8, body, 0)


def spread(lhs_ref, vals_ref, hot_ref, code_ref, first, group):
    for i in range(group):
        mask = jnp.where(code_ref[0:1, :] == (first + (i + 1)).astype(F32), 1.0, 0.0)
        mask = jnp.broadcast_to(mask, (16, mask.shape[1])).astype(BF16)
        lhs_ref[128 * i : 128 * (i + 1), :] = vals_ref[...] * jnp.concatenate([mask] * 8, axis=0)
    return lax.dot_general(lhs_ref[...], hot_ref[...], NT_DIMS, preferred_element_type=F32)


def phase_of(turn_ref, plane, a):
    ac = turn_ref[0, plane, pl.ds(a, 1), :]
    as_ = turn_ref[1, plane, pl.ds(a, 1), :]
    bc = turn_ref[2, plane]
    bs = turn_ref[3, plane]
    return ac * bc - as_ * bs, ac * bs + as_ * bc


def turned(block, turn_ref, plane):
    real, imag = [], []
    for a in range(8):
        wr, wi = phase_of(turn_ref, plane, a)
        re = block[8 * a : 8 * (a + 1)]
        im = block[64 + 8 * a : 64 + 8 * (a + 1)]
        real.append(wr * re - wi * im)
        imag.append(wi * re + wr * im)
    return jnp.concatenate(real + imag, axis=0)


def bin_planes(recv_ref, turn_ref, basis_ref, dst_ref, dst_first, turn_first, x_first, planes, scr):
    vals_ref, hot_ref, code_ref, lhs_ref = scr
    unpack(recv_ref, vals_ref, hot_ref, code_ref)
    group = 4

    def body(step, _):
        out = spread(lhs_ref, vals_ref, hot_ref, code_ref, x_first + step * group, group)
        rows = []
        for i in range(group):
            rows.append(
                turned(out[128 * i : 128 * (i + 1)], turn_ref, turn_first + step * group + i)
            )
        rows = jnp.concatenate(rows, axis=0).astype(BF16)
        res = jnp.dot(rows, basis_ref[:NY], preferred_element_type=F32)
        res = res + jnp.dot(rows, basis_ref[NY:], preferred_element_type=F32)
        for i in range(group):
            dst_ref[dst_first + step * group + i] = res[128 * i : 128 * (i + 1)]
        return 0

    lax.fori_loop(0, planes // group, body, 0)


def own_kernel(recv_ref, turn_ref, basis_ref, out_ref, *scr):
    bin_planes(recv_ref, turn_ref, basis_ref, out_ref, 0, HALO, jnp.int32(0), ROWS, scr)


BIN_SCRATCH = [
    pltpu.VMEM((128, TILES * SLOT), BF16),
    pltpu.VMEM((NY, TILES * SLOT), BF16),
    pltpu.VMEM((8, TILES * SLOT), F32),
    pltpu.VMEM((512, TILES * SLOT), BF16),
]


def own_planes(recv, turn, basis):
    return pl.pallas_call(
        own_kernel,
        out_shape=jax.ShapeDtypeStruct((ROWS, 128, NY), F32),
        in_specs=[pl.BlockSpec(memory_space=pltpu.VMEM)] * 3,
        out_specs=pl.BlockSpec(memory_space=pltpu.VMEM),
        scratch_shapes=BIN_SCRATCH,
        cost_estimate=pl.CostEstimate(
            flops=8_000_000_000, bytes_accessed=8_000_000, transcendentals=0
        ),
        compiler_params=pltpu.CompilerParams(vmem_limit_bytes=56 * 1024 * 1024),
        name="own_planes",
    )(recv, turn, basis)


def main_kernel(
    tile_ref,
    own_ref,
    left_ref,
    right_ref,
    turn_ref,
    basis_ref,
    taps_ref,
    turn1_ref,
    coef_ref,
    flat_ref,
    ext_ref,
    wave_ref,
    mid_ref,
    h_ref,
    *scr,
):
    total = ROWS + 2 * HALO
    tile = tile_ref[0]
    bin_planes(left_ref, turn_ref, basis_ref, wave_ref, 0, 0, jnp.int32(ROWS - HALO), HALO, scr)
    bin_planes(
        right_ref, turn_ref, basis_ref, wave_ref, HALO + ROWS, HALO + ROWS, jnp.int32(0), HALO, scr
    )
    wave_ref[HALO : HALO + ROWS] = own_ref[...]

    @pl.when(tile == 0)
    def _():
        wave_ref[HALO - 1] = jnp.zeros((128, NY), F32)
        for m in range(1, HALO):
            wave_ref[HALO - 1 - m] = -wave_ref[HALO - 1 + m]

    @pl.when(tile == TILES - 1)
    def _():
        edge = HALO + ROWS
        wave_ref[edge] = jnp.zeros((128, NY), F32)
        for m in range(1, HALO):
            wave_ref[edge + m] = -wave_ref[edge - m]

    def taps_body(step, _):
        re_rows = pl.ds(pl.multiple_of(step * 16, 16), 16)
        im_rows = pl.ds(pl.multiple_of(64 + step * 16, 16), 16)
        for lt in range(NY // 128):
            cols = slice(128 * lt, 128 * (lt + 1))
            for x in range(ROWS):
                c = HALO + x
                pr = taps_ref[0, 0, re_rows, cols]
                pi = taps_ref[1, 0, re_rows, cols]
                re = wave_ref[c, re_rows, cols]
                im = wave_ref[c, im_rows, cols]
                acc_r = pr * re - pi * im
                acc_i = pr * im + pi * re
                for d in range(1, HALO + 1):
                    pr = taps_ref[0, d, re_rows, cols]
                    pi = taps_ref[1, d, re_rows, cols]
                    re = wave_ref[c + d, re_rows, cols] + wave_ref[c - d, re_rows, cols]
                    im = wave_ref[c + d, im_rows, cols] + wave_ref[c - d, im_rows, cols]
                    acc_r = acc_r + (pr * re - pi * im)
                    acc_i = acc_i + (pr * im + pi * re)
                mid_ref[x, re_rows, cols] = acc_r.astype(BF16)
                mid_ref[x, im_rows, cols] = acc_i.astype(BF16)
        return 0

    lax.fori_loop(0, 4, taps_body, 0)

    h_ref[...] = jnp.zeros_like(h_ref)
    group = 4

    def depth_body(step, _):
        rows = mid_ref[pl.ds(step * group, group)].reshape(group * 128, NY)
        out = jnp.dot(rows, basis_ref[:NY], preferred_element_type=F32)
        out = out + jnp.dot(rows, basis_ref[NY:], preferred_element_type=F32)
        for i in range(group):
            x = step * group + i
            block = out[128 * i : 128 * (i + 1)]
            flat_ref[pl.ds(x, 1), :] = jnp.sum(block[:64], axis=0, keepdims=True) * (
                1.0 / math.sqrt(NF)
            )
            block = turned(block, turn1_ref, x)
            for n in range(ORDER + 1):
                acc = None
                for s in range(16):
                    w = coef_ref[n, 8 * s : 8 * (s + 1), :]
                    w = jnp.concatenate([w] * 4, axis=1)
                    term = w * block[8 * s : 8 * (s + 1)]
                    acc = term if acc is None else acc + term
                h_ref[n, pl.ds(HALO + x, 1), :] = jnp.sum(acc, axis=0, keepdims=True)
        return 0

    lax.fori_loop(0, ROWS // group, depth_body, 0)

    shape = (32, NY)
    row = lax.broadcasted_iota(jnp.int32, shape, 0)
    col = lax.broadcasted_iota(jnp.int32, shape, 1)
    grid_x = tile * ROWS - HALO + row
    inside = jnp.where((grid_x >= 0) & (grid_x < TILES * ROWS), 1.0, 0.0)
    not_first = col > 0
    not_last = col < NY - 1

    def apply_g(v):
        a = 0.5 * v + 0.25 * (pltpu.roll(v, 1, 0) + pltpu.roll(v, 31, 0))
        left = jnp.where(not_first, pltpu.roll(a, 1, 1), 0.0)
        right = jnp.where(not_last, pltpu.roll(a, NY - 1, 1), 0.0)
        return (a + 0.5 * (left + right) - v) * inside

    after = jnp.zeros(shape, F32)
    current = h_ref[ORDER]
    for n in range(ORDER - 1, 0, -1):
        after, current = current, h_ref[n] + 2.0 * apply_g(current) - after
    ext_ref[...] = (h_ref[0] + apply_g(current) - after) * (1.0 / math.sqrt(NF))


def migrate(tile, own, left, right, turn, basis, taps, turn1, coef):
    vmem = pl.BlockSpec(memory_space=pltpu.VMEM)
    return pl.pallas_call(
        main_kernel,
        out_shape=(
            jax.ShapeDtypeStruct((ROWS, NY), F32),
            jax.ShapeDtypeStruct((32, NY), F32),
        ),
        in_specs=[pl.BlockSpec(memory_space=pltpu.SMEM)] + [vmem] * 8,
        out_specs=(vmem, vmem),
        scratch_shapes=[
            pltpu.VMEM((ROWS + 2 * HALO, 128, NY), F32),
            pltpu.VMEM((ROWS, 128, NY), BF16),
            pltpu.VMEM((ORDER + 1, 32, NY), F32),
        ]
        + BIN_SCRATCH,
        cost_estimate=pl.CostEstimate(
            flops=14_000_000_000, bytes_accessed=12_000_000, transcendentals=0
        ),
        compiler_params=pltpu.CompilerParams(vmem_limit_bytes=60 * 1024 * 1024),
        name="migrate",
    )(tile, own, left, right, turn, basis, taps, turn1, coef)


def times(a, b):
    return a[0] * b[0] - a[1] * b[1], a[0] * b[1] + a[1] * b[0]


def turn_tables(delay, first):
    base_angle = first * delay
    unit = (jnp.cos(delay), jnp.sin(delay))
    powers = [(jnp.ones_like(delay), jnp.zeros_like(delay)), unit]
    for k in range(2, 9):
        powers.append(times(powers[k // 2], powers[k - k // 2]))
    eight = powers[8]
    coarse = [(jnp.cos(base_angle), jnp.sin(base_angle))]
    steps = [None, eight]
    for k in range(2, 8):
        steps.append(times(steps[k // 2], steps[k - k // 2]))
    for a in range(1, 8):
        coarse.append(times(coarse[0], steps[a]))
    fine = powers[:8]
    return jnp.stack(
        [
            jnp.stack([c[0] for c in coarse], axis=1),
            jnp.stack([c[1] for c in coarse], axis=1),
            jnp.stack([c[0] for c in fine], axis=1),
            jnp.stack([c[1] for c in fine], axis=1),
        ]
    )


def per_device(traces, bins, counts, delay, coeffs):
    tile = lax.axis_index("tile")
    freq_dev = coeffs.shape[2]
    samples = traces.shape[1]
    freq_index = lax.axis_index("freq") * freq_dev + jnp.arange(freq_dev, dtype=jnp.int32) + 1
    turns = jnp.arange(samples, dtype=jnp.int32)[:, None] * freq_index[None, :] % samples
    angle = turns.astype(F32) * (2.0 * math.pi / samples)
    table = (
        jnp.concatenate([jnp.cos(angle), -jnp.sin(angle)], axis=1) / math.sqrt(samples)
    ).astype(BF16)

    up = [(i, i + 1) for i in range(TILES - 1)]
    down = [(i + 1, i) for i in range(TILES - 1)]
    above = lax.ppermute(delay[0, ROWS - HALO :], "tile", up)
    below = lax.ppermute(delay[0, :HALO], "tile", down)
    first = (lax.axis_index("freq") * freq_dev + 1).astype(F32)
    turn = turn_tables(jnp.concatenate([above, delay[0], below], axis=0), first)
    turn1 = turn_tables(delay[1], first)

    basis = jnp.asarray(sine_basis())
    weights = jnp.asarray(shift_weights())
    taps = jnp.einsum("cnj,ndk->cdjk", coeffs, weights, precision=lax.Precision.HIGHEST)
    signed = jnp.concatenate([coeffs[0], -coeffs[1]], axis=1)
    coef = jnp.broadcast_to(signed[:, :, None], (ORDER + 1, 2 * freq_dev, 128))

    send = pack(counts, bins, traces, table)
    recv = lax.all_to_all(send, "tile", 0, 0, tiled=True)
    left = lax.ppermute(recv, "tile", up)
    right = lax.ppermute(recv, "tile", down)
    own = own_planes(recv, turn, basis)
    flat, ext = migrate(tile.reshape(1), own, left, right, turn, basis, taps, turn1, coef)

    to_up = lax.ppermute(ext[HALO + ROWS : ROWS + 2 * HALO], "tile", up)
    to_down = lax.ppermute(ext[:HALO], "tile", down)
    pad = ((0, ROWS - HALO), (0, 0))
    image = ext[HALO : HALO + ROWS] + jnp.pad(to_up, pad) + jnp.pad(to_down, ((ROWS - HALO, 0), (0, 0)))
    partial = jnp.stack([flat, image])
    count = lax.axis_size("freq")
    blocks = partial.reshape(DEPTHS, ROWS, count, NY // count).transpose(2, 0, 1, 3)
    return jnp.sum(lax.all_to_all(blocks, "freq", 0, 0, tiled=True), axis=0)


def solution(mesh):
    in_specs = (P("tile", None), P("tile"), P("tile"), P(None, "tile", None), P(None, None, "freq"))
    out_specs = P(None, "tile", "freq")
    return jax.shard_map(
        per_device, mesh=mesh, in_specs=in_specs, out_specs=out_specs, check_vma=False
    )
```

time: 468 us -> 117 us (0.25); the launches traced: 459 us -> 116 us
  other arithmetic: 193 us -> 14.2 us
  waiting for transfers between devices: 89.8 us -> 0.62 us
  starting transfers between devices: 88.9 us -> 28.6 us
  Pallas kernels: 0 us -> 46.6 us
  local copies, waits for them, and re-layouts: 47.3 us -> 10.6 us
  matrix products: 27.7 us -> 3.64 us
    sub x35 -> x8, other arithmetic: 122 us -> 6.53 us  [times(): return (a[0] * b[0] - a[1] * b[1], a[0] * b[1] + a[1] * b[0])]
    ppermute x32 -> x6, waiting for transfers between devices: 80.3 us -> 0.62 us  [the longest x1 0.6 us: per_device(): to_down = lax.ppermute(ext[:HALO], 'tile', down)]
    ppermute x32 -> x6, starting transfers between devices: 74 us -> 23 us  [the longest x1 5.75 us: per_device(): to_down = lax.ppermute(ext[:HALO], 'tile', down)]
    add x20 -> x1, other arithmetic: 50.5 us -> 0.76 us  [per_device(): ext[HALO:HALO + ROWS] + jnp.pad(to_up, pad)]
    pallas_call x0 -> x3, Pallas kernels: none -> 46.6 us  [the longest x1 30.9 us: migrate(): pl.pallas_call(main_kernel, out_shape=(jax.ShapeDtypeStruct((ROWS, NY), F...]
    dot_general x6 -> x1, matrix products: 27.7 us -> 3.64 us  [per_device(): jnp.einsum('cnj,ndk->cdjk', coeffs, weights, precision=lax.Precision.HIGH...]
    gather x2 -> x0, local copies, waits for them, and re-layouts: 19.7 us -> none  [the longest x1 13.6 us: per_device(): send_cells = padded_cells[source].reshape(tile_count, slot_cap)]
    all_to_all x2 -> x1, waiting for transfers between devices: 9.47 us -> 0.01 us  [per_device(): recv = lax.all_to_all(send, 'tile', 0, 0, tiled=True)]
  transfers between devices with their start and end apart: 34 -> 7, of which waited for: 18 -> 1; matrix products, arithmetic and copies ran while one was open for 10% -> 21% of each run, Pallas kernels for 0% -> 14%
where the time goes in v1:
time: 117 us; the launch traced here: 116 us
  Pallas kernels  46.6 us (40%)
  starting transfers between devices  28.6 us (24%)
  other arithmetic  14.2 us (12%)
  local copies, waits for them, and re-layouts  10.6 us (9%)
  blocking collectives  10.6 us (9%)
  matrix products  3.64 us (3%)
    pallas_call x1, Pallas kernels, migrate(): pl.pallas_call(main_kernel, out_shape=(jax.ShapeDtypeStruct((ROWS, NY), F...  30.9 us
    pallas_call x1, Pallas kernels, own_planes(): pl.pallas_call(own_kernel, out_shape=jax.ShapeDtypeStruct((ROWS, 128, NY)...  11.9 us
    all_to_all x1, blocking collectives, per_device(): return jnp.sum(lax.all_to_all(blocks, 'freq', 0, 0, tiled=True), axis=0)  10.6 us
    sub x8, other arithmetic, times(): return (a[0] * b[0] - a[1] * b[1], a[0] * b[1] + a[1] * b[0])  6.53 us
    ppermute x1, starting transfers between devices, per_device(): to_down = lax.ppermute(ext[:HALO], 'tile', down)  5.75 us
    ppermute x1, starting transfers between devices, per_device(): below = lax.ppermute(delay[0, :HALO], 'tile', down)  5.75 us
    ppermute x1, starting transfers between devices, per_device(): right = lax.ppermute(recv, 'tile', down)  5.65 us
    all_to_all x1, starting transfers between devices, per_device(): recv = lax.all_to_all(send, 'tile', 0, 0, tiled=True)  5.57 us
  transfers between devices with their start and end apart: 7, of which 1 were waited for; matrix products, arithmetic and copies ran while one was open for 21% of the time, Pallas kernels for 14%

profile of v1, /device:TPU:8, one launch (start us, length us, event | category | flops | bytes accessed | tf_op | source)
XLA Modules:
  0.0 115.9 jit_solution(622650959110013387)
XLA Ops:
  0.0 0.9 fusion.12
  1.0 1.9 %collective-permute-start = (f32[8,512]{1,0:T(8,128)S(1)}, f32[8,512]{1,0:T(8,128)S(1)}, u32[]{:S(2)}, u32[]{:S(2)}) collective-permute-start(f32[8,512]{1,0:T(8,128)S(1)} %bitcast.73), channel_id=1, source_target_pairs={{0,1},{1,2},{2,3},{3,4},{4,5},{5,6},{6,7},{7,8},{8,9},{9,10},{10,1... | collective-permute-start | bytes 49160 | tf_op jit(solution)/shard_map/ppermute | solution.py:402
  2.9 5.8 %collective-permute-start.1 = (f32[8,512]{1,0:T(8,128)S(1)}, f32[8,512]{1,0:T(8,128)S(1)}, u32[]{:S(2)}, u32[]{:S(2)}) collective-permute-start(f32[8,512]{1,0:T(8,128)S(1)} %bitcast.74), channel_id=1, source_target_pairs={{1,0},{2,1},{3,2},{4,3},{5,4},{6,5},{7,6},{8,7},{9,8},{10,9},{11,1... | collective-permute-start | bytes 49160 | tf_op jit(solution)/shard_map/ppermute | solution.py:403
  8.7 2.1 %fusion.7 = (f32[1024,64]{1,0:T(8,128)S(1)}, f32[1024,64]{1,0:T(8,128)S(1)}) fusion(s32[64]{0:T(128)S(1)} %add_add_fusion), kind=kLoop, calls=%fused_computation.15 | loop fusion | flops 983040 | bytes 524544 | tf_op jit(solution)/shard_map/cos | solution.py:397
  11.7 3.8 %pack_traces.1 = bf16[32,96,128]{2,1,0:T(8,128)(2,1)} custom-call(s32[1]{0:T(128)S(6)} %copy.55.count_ref, s32[1,1024]{1,0:T(1,128)S(1)} %bitcast.63, bf16[1024,1024]{1,0:T(8,128)(2,1)S(1)} %copy-done, bf16[1024,128]{1,0:T(8,128)(2,1)S(1)} %fusion.3.table_ref), custom_call_target="tpu_custom_call" | custom-call | flops 3000000000 | bytes 4000000 | tf_op jit(solution)/shard_map/pack_traces/pallas_call | solution.py:105
  15.5 5.6 %all-to-all-start = ((bf16[32,96,128]{2,1,0:T(8,128)(2,1)}), bf16[32,96,128]{2,1,0:T(8,128)(2,1)S(1)}, u32[]{:S(2)}, u32[]{:S(2)}) async-start(bf16[32,96,128]{2,1,0:T(8,128)(2,1)} %pack_traces.1), calls=%async_computation | async-start | bytes 1572864 | tf_op jit(solution)/shard_map/all_to_all | solution.py:415
  21.8 1.7 %multiply_subtract_fusion.24 = (f32[12,1,512]{2,1,0:T(1,128)S(1)}, f32[12,1,512]{2,1,0:T(1,128)S(1)}, f32[12,1,512]{2,1,0:T(1,128)S(1)}, f32[12,1,512]{2,1,0:T(1...) fusion(f32[2,12,512]{2,0,1:T(2,128)S(1)} %copy-done.3, ...), kind=kLoop, calls=%fused_computation.82 | loop fusion | flops 251904 | bytes 442372 | tf_op jit(solution)/shard_map/sub | solution.py:362
  23.6 3.6 %convolution_bitcast_fusion.taps_ref = f32[2,9,64,512]{3,2,1,0:T(8,128)} fusion(f32[9,9,512,1]{2,0,1,3:T(8,128)S(1)} %copy-done.4, f32[2,9,64,1]{2,0,1,3:T(2,128)S(1)} %bitcast.72), kind=kOutput, calls=%fused_computation.1 | convolution fusion | flops 63700992 | bytes 2529792 | tf_op jit(solution)/shard_map/cnj,ndk->cdjk/dot_general | solution.py:410
  29.7 1.0 pad_maximum_fusion.1.turn1_ref
  30.8 1.5 %fusion.10 = (f32[28,1,512]{2,1,0:T(1,128)S(1)}, f32[28,1,512]{2,1,0:T(1,128)S(1)}) fusion(f32[8,1,512]{2,1,0:T(1,128)S(1)} %concatenate.268, f32[12,1,512]{2,1,0:T(1,128)S(1)} %get-tuple-element.111, f32[8,1,512]{2,1,0:T(1,128)S(1)} %concatenate.266), kind=kLoop, calls=%fused_computation.114 | loop fusion | flops 28672 | bytes 172032 | tf_op jit(solution)/shard_map/cos | solution.py:367
  32.3 1.5 %sin.370 = f32[28,1,512]{2,1,0:T(1,128)S(1)} sine(f32[28,1,512]{2,1,0:T(1,128)S(1)} %get-tuple-element.56) | non-fusion elementwise | bytes 114688 | tf_op jit(solution)/shard_map/sin | solution.py:367
  33.8 2.3 %multiply_subtract_fusion.4 = (f32[28,1,512]{2,1,0:T(1,128)S(1)}, f32[28,1,512]{2,1,0:T(1,128)S(1)}, f32[28,1,512]{2,1,0:T(1,128)S(1)}, f32[28,1,512]{2,1,0:T(1,...) fusion(f32[28,1,512]{2,1,0:T(1,128)S(1)} %get-tuple-element.56,, ...), kind=kLoop, calls=%fused_computation.38 | loop fusion | flops 587776 | bytes 1146884 | tf_op jit(solution)/shard_map/sub | solution.py:362
  39.0 1.0 stack.42
  40.7 2.0 %collective-permute-start.2 = (bf16[32,96,128]{2,1,0:T(8,128)(2,1)S(1)}, bf16[32,96,128]{2,1,0:T(8,128)(2,1)S(1)}, u32[]{:S(2)}, u32[]{:S(2)}) collective-permute-start(bf16[32,96,128]{2,1,0:T(8,128)(2,1)S(1)} %all-to-all-done.recv_ref), channel_id=1, source_target_pairs={{0,1},{1,2},{2,3},{3,4},{4,5},{5,6},{6,7},{7,8},{8,9},{9,10},{10,1... | collective-permute-start | bytes 2359304 | tf_op jit(solution)/shard_map/ppermute | solution.py:416
  42.7 5.6 %collective-permute-start.3 = (bf16[32,96,128]{2,1,0:T(8,128)(2,1)S(1)}, bf16[32,96,128]{2,1,0:T(8,128)(2,1)S(1)}, u32[]{:S(2)}, u32[]{:S(2)}) collective-permute-start(bf16[32,96,128]{2,1,0:T(8,128)(2,1)S(1)} %all-to-all-done.recv_ref), channel_id=1, source_target_pairs={{1,0},{2,1},{3,2},{4,3},{5,4},{6,5},{7,6},{8,7},{9,8},{10,9},{11,1... | collective-permute-start | bytes 2359304 | tf_op jit(solution)/shard_map/ppermute | solution.py:417
  48.4 1.4 %pad_maximum_fusion.turn_ref = f32[4,28,8,512]{3,2,1,0:T(8,128)} fusion(f32[1,28,8,512]{3,2,1,0:T(8,128)S(1)} %bitcast.65, f32[1,28,8,512]{3,2,1,0:T(8,128)S(1)} %bitcast.64, f32[1,28,8,512]{3,2,1,0:T(8,128)S(1)} %bitcast.67, f32[1,28,8,512]{3,2,1,0:T(8,128)S(1)} %bitcast.66), kind=kLoop, calls=%fused_computation | loop fusion | flops 1376256 | bytes 3670016 | tf_op jit(solution)/shard_map/stack | solution.py:379
  49.8 11.9 %own_planes.1.own_ref = f32[12,128,512]{2,1,0:T(8,128)} custom-call(bf16[32,96,128]{2,1,0:T(8,128)(2,1)} %copy-done.2, f32[4,28,8,512]{3,2,1,0:T(8,128)} %pad_maximum_fusion.turn_ref, bf16[1024,512]{1,0:T(8,128)(2,1)} %constant.47.clone.basis_ref), custom_call_target="tpu_custom_call" | custom-call | flops 8000000000 | bytes 8000000 | tf_op jit(solution)/shard_map/own_planes/pallas_call | solution.py:212
  61.7 1.3 %broadcast_in_dim.2.coef_ref = f32[9,128,128]{2,1,0:T(8,128)} broadcast(f32[9,128]{1,0:T(8,128)S(1)} %pad_maximum_fusion.3), dimensions={0,1} | broadcast | bytes 594432 | tf_op jit(solution)/shard_map/broadcast_in_dim | solution.py:412
  63.1 30.9 %migrate.1 = (f32[12,512]{1,0:T(8,128)}, f32[32,512]{1,0:T(8,128)}) custom-call(s32[1]{0:T(128)} %bitcast.tile_ref, f32[12,128,512]{2,1,0:T(8,128)} %own_planes.1.own_ref, bf16[32,96,128]{2,1,0:T(8,128)(2,1)} %copy-done.6, bf16[32,96,128]{2,1,0:T(8,128)(2,1)} %copy-done.7, f32[4,28,8,512]{3,2,1,0:T(8,128)} %pad_maximum_fusion.turn_ref, ...), custom_call_target="tpu_custom_call" | custom-call | flops 14000000000 | bytes 12000000 | tf_op jit(solution)/shard_map/migrate/pallas_call | solution.py:339
  94.7 1.9 %collective-permute-start.4 = (f32[8,512]{1,0:T(8,128)S(1)}, f32[8,512]{1,0:T(8,128)S(1)}, u32[]{:S(2)}, u32[]{:S(2)}) collective-permute-start(f32[8,512]{1,0:T(8,128)S(1)} %get-tuple-element.97), channel_id=1, source_target_pairs={{0,1},{1,2},{2,3},{3,4},{4,5},{5,6},{6,7},{7,8},{8,9},{9,10},{10,1... | collective-permute-start | bytes 49160 | tf_op jit(solution)/shard_map/ppermute | solution.py:421
  96.6 5.8 %collective-permute-start.5 = (f32[8,512]{1,0:T(8,128)S(1)}, f32[8,512]{1,0:T(8,128)S(1)}, u32[]{:S(2)}, u32[]{:S(2)}) collective-permute-start(f32[8,512]{1,0:T(8,128)S(1)} %get-tuple-element.98), channel_id=1, source_target_pairs={{1,0},{2,1},{3,2},{4,3},{5,4},{6,5},{7,6},{8,7},{9,8},{10,9},{11,1... | collective-permute-start | bytes 49160 | tf_op jit(solution)/shard_map/ppermute | solution.py:422
  102.4 0.8 stack.60
  103.8 0.8 pad_add_fusion
  104.7 10.6 %all_to_all.10 = f32[4,2,12,128]{3,1,2,0:T(2,128)S(1)} all-to-all(f32[4,2,12,128]{3,1,2,0:T(2,128)S(1)} %maximum_bitcast_fusion), channel_id=1, replica_groups=mesh['freq'=4,'tile'=32] {'freq'}, dimensions={0} | all-to-all | bytes 98304 | tf_op jit(solution)/shard_map/all_to_all | solution.py:428
  (56 shorter events, 9.2 us)
Async XLA Ops:
  0.0 11.6 %copy-start.1 = (s32[1024]{0:T(1024)S(1)}, s32[1024]{0:T(1024)}, u32[]{:S(2)}) copy-start(s32[1024]{0:T(1024)} %param.8) | copy-start | bytes 12292
  0.0 11.6 %copy-start = (bf16[1024,1024]{1,0:T(8,128)(2,1)S(1)}, bf16[1024,1024]{1,0:T(8,128)(2,1)}, u32[]{:S(2)}) copy-start(bf16[1024,1024]{1,0:T(8,128)(2,1)} %traces_ref.1) | copy-start | bytes 6291460
  1.0 29.8 %collective-permute-start = (f32[8,512]{1,0:T(8,128)S(1)}, f32[8,512]{1,0:T(8,128)S(1)}, u32[]{:S(2)}, u32[]{:S(2)}) collective-permute-start(f32[8,512]{1,0:T(8,128)S(1)} %bitcast.73), channel_id=1, source_target_pairs={{0,1},{1,2},{2,3},{3,4},{4,5},{5,6},{6,7},{7,8},{8,9},{9,10},{10,1... | collective-permute-start | bytes 49160 | tf_op jit(solution)/shard_map/ppermute | solution.py:402
  2.9 27.9 %collective-permute-start.1 = (f32[8,512]{1,0:T(8,128)S(1)}, f32[8,512]{1,0:T(8,128)S(1)}, u32[]{:S(2)}, u32[]{:S(2)}) collective-permute-start(f32[8,512]{1,0:T(8,128)S(1)} %bitcast.74), channel_id=1, source_target_pairs={{1,0},{2,1},{3,2},{4,3},{5,4},{6,5},{7,6},{8,7},{9,8},{10,9},{11,1... | collective-permute-start | bytes 49160 | tf_op jit(solution)/shard_map/ppermute | solution.py:403
  11.6 9.4 %copy-start.3 = (f32[2,12,512]{2,0,1:T(2,128)S(1)}, f32[2,12,512]{2,0,1:T(2,128)}, u32[]{:S(2)}) copy-start(f32[2,12,512]{2,0,1:T(2,128)} %param.10) | copy-start | bytes 147460
  15.5 8.0 %copy-start.5 = (f32[2,9,64]{2,0,1:T(2,128)S(1)}, f32[2,9,64]{2,0,1:T(2,128)}, u32[]{:S(2)}) copy-start(f32[2,9,64]{2,0,1:T(2,128)} %param.11) | copy-start | bytes 13828
  15.5 8.1 %copy-start.4 = (f32[9,9,512,1]{2,0,1,3:T(8,128)S(1)}, f32[9,9,512,1]{2,0,1,3:T(8,128)}, u32[]{:S(2)}) copy-start(f32[9,9,512,1]{2,0,1,3:T(8,128)} %constant.55) | copy-start | bytes 497668
  15.5 25.1 %all-to-all-start = ((bf16[32,96,128]{2,1,0:T(8,128)(2,1)}), bf16[32,96,128]{2,1,0:T(8,128)(2,1)S(1)}, u32[]{:S(2)}, u32[]{:S(2)}) async-start(bf16[32,96,128]{2,1,0:T(8,128)(2,1)} %pack_traces.1), calls=%async_computation | async-start | bytes 1572864 | tf_op jit(solution)/shard_map/all_to_all | solution.py:415
  40.7 9.1 %copy-start.2 = (bf16[32,96,128]{2,1,0:T(8,128)(2,1)}, bf16[32,96,128]{2,1,0:T(8,128)(2,1)S(1)}, u32[]{:S(2)}) copy-start(bf16[32,96,128]{2,1,0:T(8,128)(2,1)S(1)} %all-to-all-done.recv_ref) | copy-start | bytes 2359300
  40.7 21.0 %collective-permute-start.2 = (bf16[32,96,128]{2,1,0:T(8,128)(2,1)S(1)}, bf16[32,96,128]{2,1,0:T(8,128)(2,1)S(1)}, u32[]{:S(2)}, u32[]{:S(2)}) collective-permute-start(bf16[32,96,128]{2,1,0:T(8,128)(2,1)S(1)} %all-to-all-done.recv_ref), channel_id=1, source_target_pairs={{0,1},{1,2},{2,3},{3,4},{4,5},{5,6},{6,7},{7,8},{8,9},{9,10},{10,1... | collective-permute-start | bytes 2359304 | tf_op jit(solution)/shard_map/ppermute | solution.py:416
  42.7 18.9 %collective-permute-start.3 = (bf16[32,96,128]{2,1,0:T(8,128)(2,1)S(1)}, bf16[32,96,128]{2,1,0:T(8,128)(2,1)S(1)}, u32[]{:S(2)}, u32[]{:S(2)}) collective-permute-start(bf16[32,96,128]{2,1,0:T(8,128)(2,1)S(1)} %all-to-all-done.recv_ref), channel_id=1, source_target_pairs={{1,0},{2,1},{3,2},{4,3},{5,4},{6,5},{7,6},{8,7},{9,8},{10,9},{11,1... | collective-permute-start | bytes 2359304 | tf_op jit(solution)/shard_map/ppermute | solution.py:417
  61.7 1.3 %copy-start.6 = (bf16[32,96,128]{2,1,0:T(8,128)(2,1)}, bf16[32,96,128]{2,1,0:T(8,128)(2,1)S(1)}, u32[]{:S(2)}) copy-start(bf16[32,96,128]{2,1,0:T(8,128)(2,1)S(1)} %collective-permute-done.2.left_ref) | copy-start | bytes 2359300
  61.7 1.4 %copy-start.7 = (bf16[32,96,128]{2,1,0:T(8,128)(2,1)}, bf16[32,96,128]{2,1,0:T(8,128)(2,1)S(1)}, u32[]{:S(2)}) copy-start(bf16[32,96,128]{2,1,0:T(8,128)(2,1)S(1)} %collective-permute-done.3.right_ref) | copy-start | bytes 2359300
  94.7 8.5 %collective-permute-start.4 = (f32[8,512]{1,0:T(8,128)S(1)}, f32[8,512]{1,0:T(8,128)S(1)}, u32[]{:S(2)}, u32[]{:S(2)}) collective-permute-start(f32[8,512]{1,0:T(8,128)S(1)} %get-tuple-element.97), channel_id=1, source_target_pairs={{0,1},{1,2},{2,3},{3,4},{4,5},{5,6},{6,7},{7,8},{8,9},{9,10},{10,1... | collective-permute-start | bytes 49160 | tf_op jit(solution)/shard_map/ppermute | solution.py:421
  96.6 7.2 %collective-permute-start.5 = (f32[8,512]{1,0:T(8,128)S(1)}, f32[8,512]{1,0:T(8,128)S(1)}, u32[]{:S(2)}, u32[]{:S(2)}) collective-permute-start(f32[8,512]{1,0:T(8,128)S(1)} %get-tuple-element.98), channel_id=1, source_target_pairs={{1,0},{2,1},{3,2},{4,3},{5,4},{6,5},{7,6},{8,7},{9,8},{10,9},{11,1... | collective-permute-start | bytes 49160 | tf_op jit(solution)/shard_map/ppermute | solution.py:422
